TPU v7x, 32 devices: a whole 2x2x4 slice. The times are simulated.
32 devices in a mesh: strike: 8 (over y, x, core), dip: 4 (over z).
Axes of the slice: x: 2, y: 2, z: 4, core: 2. Of those that a mesh axis runs over, the one named last changes fastest.
Arguments:
- slip: float32 [8192, 2048], P('strike', 'dip'), may hold values from -4 to 8
- slip_rate: float32 [8192, 2048], P('strike', 'dip'), may hold values from -6 to 6
- state: float32 [8192, 2048], P('strike', 'dip'), may hold values from -1 to 1
- loading: float32 [8192, 2048], P('strike', 'dip'), may hold values from -8 to 8
- normal_stress: float32 [8192, 2048], P('strike', 'dip'), may hold values from 0.5 to 2
- patch: int32 [8192, 2048], P('strike', 'dip'), may hold values from 0 to 3
- rate_coef: float32 [4], replicated, may hold values from 0.3 to 1
- state_coef: float32 [4], replicated, may hold values from 0.3 to 1
- slip_scale: float32 [4], replicated, may hold values from 0.5 to 2
- kernel: bfloat16 [16, 2048, 8192], P(None, ('strike', 'dip')), may hold values from -1.5 to 1.5
- history: bfloat16 [16, 2, 2048, 8192], P(None, None, ('strike', 'dip')), may hold values from -6 to 6
Outputs:
- new_rate: float32 [8192, 2048], P('strike', 'dip')
- new_state: float32 [8192, 2048], P('strike', 'dip')
- transfer_stress: float32 [8192, 2048], P('strike', 'dip')
- rate_modes: bfloat16 [2, 2048, 8192], P(None, ('strike', 'dip'))
All inputs are finite; a program needn't handle non-finite values.
Results may differ from a plain program's by a relative error of at most 0.001.
Values sent between devices are 32-bit elements; how exact they have to be, the bound alone decides.
A program may use at most 192 MiB of HBM per device.

v0:
```python
import math
import jax
import jax.numpy as jnp
from jax import lax
from jax.sharding import PartitionSpec as P

NEWTON = 8
shear_modulus = 1.0
damping = 0.5
relaxation = 0.35
time_step = 0.1


def inverse_sinh(value):
    size_v = jnp.abs(value)
    square = size_v * size_v
    result = jnp.log1p(size_v + square / (1.0 + jnp.sqrt(square + 1.0)))
    return jnp.where(value < 0.0, -result, result)


def tables(count_in, count_out, modulus, sign):
    row_index = lax.broadcasted_iota(jnp.int32, (count_in, count_out), 0)
    col_index = lax.broadcasted_iota(jnp.int32, (count_in, count_out), 1)
    angles = 2.0 * math.pi / modulus * (row_index * col_index % modulus).astype(jnp.float32)
    return (jnp.cos(angles), sign * jnp.sin(angles))


def cproduct(pattern, part_re, part_im, table_re, table_im):

    def product(left_op, right_op):
        return jnp.einsum(pattern, left_op, right_op, precision=lax.Precision.HIGHEST)

    if part_im is None:
        return (product(part_re, table_re), product(part_re, table_im))
    return (
        product(part_re, table_re) - product(part_im, table_im),
        product(part_re, table_im) + product(part_im, table_re),
    )


def factors(length):
    inner_len = 128
    return (length // inner_len, inner_len)


def transform_rows(part_re, part_im, sign, flipped):
    row_count, length = part_re.shape
    outer_len, inner_len = factors(length)
    part_re = part_re.reshape(row_count, outer_len, inner_len)
    if part_im is not None:
        part_im = part_im.reshape(row_count, outer_len, inner_len)
    first_re, first_im = tables(outer_len, outer_len, outer_len, sign)
    part_re, part_im = cproduct("rab,ac->rcb", part_re, part_im, first_re, first_im)
    twist_re, twist_im = tables(outer_len, inner_len, length, sign)
    part_re, part_im = (
        part_re * twist_re - part_im * twist_im,
        part_re * twist_im + part_im * twist_re,
    )
    second_re, second_im = tables(inner_len, inner_len, inner_len, sign)
    pattern = "rcb,bm->mcr" if flipped else "rcb,bm->rmc"
    part_re, part_im = cproduct(pattern, part_re, part_im, second_re, second_im)
    out_shape = (length, row_count) if flipped else (row_count, length)
    factor = 1.0 / math.sqrt(length)
    return (part_re.reshape(out_shape) * factor, part_im.reshape(out_shape) * factor)


def transform_cols(part_re, part_im, sign):
    length, col_count = part_re.shape
    outer_len, inner_len = factors(length)
    part_re = part_re.reshape(outer_len, inner_len, col_count)
    part_im = part_im.reshape(outer_len, inner_len, col_count)
    first_re, first_im = tables(outer_len, outer_len, outer_len, sign)
    part_re, part_im = cproduct("abr,ac->cbr", part_re, part_im, first_re, first_im)
    twist_re, twist_im = tables(outer_len, inner_len, length, sign)
    twist_re = twist_re[:, :, None]
    twist_im = twist_im[:, :, None]
    part_re, part_im = (
        part_re * twist_re - part_im * twist_im,
        part_re * twist_im + part_im * twist_re,
    )
    second_re, second_im = tables(inner_len, inner_len, inner_len, sign)
    part_re, part_im = cproduct("cbr,bm->rmc", part_re, part_im, second_re, second_im)
    factor = 1.0 / math.sqrt(length)
    return (
        part_re.reshape(col_count, length) * factor,
        part_im.reshape(col_count, length) * factor,
    )


def wavenumber(index, count):
    return 2.0 * math.pi / count * ((index + count // 2) % count - count // 2).astype(jnp.float32)


def lookup(patch, table):
    result = jnp.zeros(patch.shape, jnp.float32)
    for label in range(table.shape[0]):
        result = jnp.where(patch == label, table[label], result)
    return result


def friction(slip_rate, state, loading, normal_stress, transfer, coef_a, coef_b, length_l):
    stress = loading + transfer
    prefix = 2.0 * jnp.exp(-state / coef_a)
    angle_w = inverse_sinh(slip_rate / prefix)
    for iteration in range(NEWTON):
        residue = normal_stress * coef_a * angle_w + damping * prefix * jnp.sinh(angle_w) - stress
        slope = normal_stress * coef_a + damping * prefix * jnp.cosh(angle_w)
        ratio = residue / slope
        angle_w = angle_w - relaxation * ratio / (1.0 + jnp.abs(ratio))
    new_rate = prefix * jnp.sinh(angle_w)
    new_state = state + time_step * (coef_b / length_l) * (
        jnp.exp(-state / coef_b) - jnp.abs(new_rate)
    )
    return (new_rate, new_state)


def per_device(
    slip,
    slip_rate,
    state,
    loading,
    normal_stress,
    patch,
    rate_coef,
    state_coef,
    slip_scale,
    kernel,
    history,
):
    strike_count = lax.axis_size("strike")
    dip_count = lax.axis_size("dip")
    slip_rows, rate_rows = (
        lax.all_to_all(slip, "dip", split_axis=0, concat_axis=1, tiled=True),
        lax.all_to_all(slip_rate, "dip", split_axis=0, concat_axis=1, tiled=True),
    )
    slip_re, slip_im = transform_rows(slip_rows, None, -1.0, True)
    rate_re, rate_im = transform_rows(rate_rows, None, -1.0, True)
    pieces = (
        lax.all_to_all(slip_re, ("strike", "dip"), split_axis=0, concat_axis=1, tiled=True),
        lax.all_to_all(slip_im, ("strike", "dip"), split_axis=0, concat_axis=1, tiled=True),
        lax.all_to_all(rate_re, ("strike", "dip"), split_axis=0, concat_axis=1, tiled=True),
        lax.all_to_all(rate_im, ("strike", "dip"), split_axis=0, concat_axis=1, tiled=True),
    )
    slip_re, slip_im = transform_rows(pieces[0], pieces[1], -1.0, False)
    rate_re, rate_im = transform_rows(pieces[2], pieces[3], -1.0, False)
    band, total_x = slip_re.shape
    total_y = band * strike_count * dip_count
    offset = (lax.axis_index("strike") * dip_count + lax.axis_index("dip")) * band
    wave_y = wavenumber(offset + lax.broadcasted_iota(jnp.int32, (band,), 0), total_y)
    wave_x = wavenumber(lax.broadcasted_iota(jnp.int32, (total_x,), 0), total_x)
    magnitude = jnp.sqrt(wave_y[:, None] ** 2 + wave_x[None, :] ** 2)
    memory_re = jnp.einsum("jrc,jrc->rc", kernel, history[:, 0], preferred_element_type=jnp.float32)
    memory_im = jnp.einsum("jrc,jrc->rc", kernel, history[:, 1], preferred_element_type=jnp.float32)
    static = -0.5 * shear_modulus * magnitude
    stress_re = static * slip_re + memory_re
    stress_im = static * slip_im + memory_im
    rate_modes = jnp.stack([rate_re, rate_im]).astype(jnp.bfloat16)
    back_re, back_im = transform_rows(stress_re, stress_im, 1.0, False)
    back = (
        lax.all_to_all(back_re, ("strike", "dip"), split_axis=1, concat_axis=0, tiled=True),
        lax.all_to_all(back_im, ("strike", "dip"), split_axis=1, concat_axis=0, tiled=True),
    )
    line_re, line_im = transform_cols(back[0], back[1], 1.0)
    transfer = lax.all_to_all(line_re, "dip", split_axis=1, concat_axis=0, tiled=True)
    coef_a = lookup(patch, rate_coef)
    coef_b = lookup(patch, state_coef)
    length_l = lookup(patch, slip_scale)
    new_rate, new_state = friction(
        slip_rate, state, loading, normal_stress, transfer, coef_a, coef_b, length_l
    )
    return (new_rate, new_state, transfer, rate_modes)


def solution(mesh):
    return jax.shard_map(
        per_device,
        mesh=mesh,
        in_specs=(
            P("strike", "dip"),
            P("strike", "dip"),
            P("strike", "dip"),
            P("strike", "dip"),
            P("strike", "dip"),
            P("strike", "dip"),
            P(),
            P(),
            P(),
            P(None, ("strike", "dip"), None),
            P(None, None, ("strike", "dip"), None),
        ),
        out_specs=(
            P("strike", "dip"),
            P("strike", "dip"),
            P("strike", "dip"),
            P(None, ("strike", "dip"), None),
        ),
        check_vma=False,
    )
```

profile of v0, /device:TPU:0, one launch (start us, length us, event | category | flops | bytes accessed | tf_op | source)
XLA Modules:
  0.0 581.7 jit_solution(3470144887140389631)
XLA Ops:
  0.6 54.6 %all_to_all.126 = f32[4,256,512]{2,1,0:T(8,128)S(1)} all-to-all(f32[4,256,512]{2,1,0:T(8,128)} %bitcast.262), channel_id=1, replica_groups=mesh['strike'=8,'dip'=4] {'dip'}, dimensions={0} | all-to-all | bytes 4194304 | tf_op jit(solution)/shard_map/all_to_all | solution.py:134
  71.0 36.1 %all-to-all-done = f32[4,256,512]{2,1,0:T(8,128)} async-done(((f32[4,256,512]{2,1,0:T(8,128)}), f32[4,256,512]{2,1,0:T(8,128)}, u32[]{:S(2)}, u32[]{:S(2)}) %all-to-all-start) | async-done | bytes 2097184 | tf_op jit(solution)/shard_map/all_to_all | solution.py:133
  116.9 5.5 subtract_bitcast_fusion
  144.2 37.2 %all-to-all-done.2 = f32[32,64,256]{2,1,0:T(8,128)} async-done(((f32[32,64,256]{2,1,0:T(8,128)}), f32[32,64,256]{2,1,0:T(8,128)}, u32[]{:S(2)}, u32[]{:S(2)}) %all-to-all-start.2) | async-done | bytes 2097184 | tf_op jit(solution)/shard_map/all_to_all | solution.py:140
  181.3 4.7 all-to-all-start.1
  195.9 36.8 %all-to-all-done.1 = f32[32,64,256]{2,1,0:T(8,128)} async-done(((f32[32,64,256]{2,1,0:T(8,128)}), f32[32,64,256]{2,1,0:T(8,128)}, u32[]{:S(2)}, u32[]{:S(2)}) %all-to-all-start.1) | async-done | bytes 2097184 | tf_op jit(solution)/shard_map/all_to_all | solution.py:139
  232.7 5.2 all-to-all-start.7
  237.9 20.0 %fusion.1 = (f32[64,8192]{1,0:T(8,128)}, f32[64,8192]{1,0:T(8,128)}) fusion(bf16[16,64,8192]{2,1,0:T(8,128)(2,1)} %param.20, bf16[16,2,64,8192]{3,2,1,0:T(8,128)(2,1)} %param.21), kind=kLoop, calls=%fused_computation.3 | loop fusion | flops 57671680 | bytes 54525952 | tf_op jit(solution)/shard_map/jrc,jrc->rc/dot_general | solution.py:153
  287.7 6.3 %all-to-all-start.8 = ((f32[32,64,256]{2,1,0:T(8,128)}), f32[32,64,256]{2,1,0:T(8,128)}, u32[]{:S(2)}, u32[]{:S(2)}) async-start(f32[32,64,256]{2,1,0:T(8,128)} %bitcast.255), calls=%async_computation.8 | async-start | bytes 4194304 | tf_op jit(solution)/shard_map/all_to_all | solution.py:142
  305.3 4.8 mul.985
  321.4 5.3 mul.989
  349.7 4.8 mul.1001
  358.7 6.1 %all-to-all-start.4 = ((f32[64,32,256]{2,0,1:T(8,128)}), f32[64,32,256]{2,0,1:T(8,128)}, u32[]{:S(2)}, u32[]{:S(2)}) async-start(f32[64,32,256]{2,0,1:T(8,128)} %copy.149), calls=%async_computation.4 | async-start | bytes 4194304 | tf_op jit(solution)/shard_map/all_to_all | solution.py:161
  382.1 29.6 %all-to-all-done.4 = f32[64,32,256]{2,0,1:T(8,128)} async-done(((f32[64,32,256]{2,0,1:T(8,128)}), f32[64,32,256]{2,0,1:T(8,128)}, u32[]{:S(2)}, u32[]{:S(2)}) %all-to-all-start.4) | async-done | bytes 2097184 | tf_op jit(solution)/shard_map/all_to_all | solution.py:161
  411.7 4.7 all-to-all-start.3
  426.6 4.9 copy.173
  438.8 5.7 fusion.91
  444.5 5.7 fusion.89
  450.2 12.8 %all-to-all-done.3 = f32[64,32,256]{2,0,1:T(8,128)} async-done(((f32[64,32,256]{2,0,1:T(8,128)}), f32[64,32,256]{2,0,1:T(8,128)}, u32[]{:S(2)}, u32[]{:S(2)}) %all-to-all-start.3) | async-done | bytes 2097184 | tf_op jit(solution)/shard_map/all_to_all | solution.py:160
  463.0 5.5 fusion.109
  468.5 5.3 multiply_subtract_fusion.1
  483.0 5.3 all-to-all-start.5
  517.3 20.5 %all-to-all-done.5 = f32[256,4,512]{0,2,1:T(8,128)} async-done(((f32[256,4,512]{0,2,1:T(8,128)}), f32[256,4,512]{0,2,1:T(8,128)}, u32[]{:S(2)}, u32[]{:S(2)}) %all-to-all-start.5) | async-done | bytes 2097184 | tf_op jit(solution)/shard_map/all_to_all | solution.py:164
  540.8 40.4 %multiply_add_fusion.1 = (f32[1024,512]{1,0:T(8,128)}, f32[1024,512]{1,0:T(8,128)}) fusion(f32[1024,512]{1,0:T(8,128)} %param.13, pred[1024,512]{1,0:T(8,128)(4,1)} %get-tuple-element.16, pred[1024,512]{1,0:T(8,128)(4,1)S(1)} %copy-done.22, pred[1024,512]{1,0:T(8,128)(4,1)} %get-tuple-element.17, pred[1024,512]{1,0:T(8,128)(4,1)S(1)} %copy-done.21, ...), kind=kLoop, calls=%fused_computation.102 | loop fusion | flops 120061952 | bytes 16777264 | tf_op jit(solution)/shard_map/add | solution.py:111
  (137 shorter events, 212.1 us)
Async XLA Ops:
  55.2 51.9 %all-to-all-start = ((f32[4,256,512]{2,1,0:T(8,128)}), f32[4,256,512]{2,1,0:T(8,128)}, u32[]{:S(2)}, u32[]{:S(2)}) async-start(f32[4,256,512]{2,1,0:T(8,128)} %bitcast.261), calls=%async_computation | async-start | bytes 4194304 | tf_op jit(solution)/shard_map/all_to_all | solution.py:133
  130.4 50.9 %all-to-all-start.2 = ((f32[32,64,256]{2,1,0:T(8,128)}), f32[32,64,256]{2,1,0:T(8,128)}, u32[]{:S(2)}, u32[]{:S(2)}) async-start(f32[32,64,256]{2,1,0:T(8,128)} %bitcast.259), calls=%async_computation.2 | async-start | bytes 4194304 | tf_op jit(solution)/shard_map/all_to_all | solution.py:140
  134.5 4.4 copy-start.7
  181.3 51.4 %all-to-all-start.1 = ((f32[32,64,256]{2,1,0:T(8,128)}), f32[32,64,256]{2,1,0:T(8,128)}, u32[]{:S(2)}, u32[]{:S(2)}) async-start(f32[32,64,256]{2,1,0:T(8,128)} %bitcast.256), calls=%async_computation.1 | async-start | bytes 4194304 | tf_op jit(solution)/shard_map/all_to_all | solution.py:139
  232.7 55.0 %all-to-all-start.7 = ((f32[32,64,256]{2,1,0:T(8,128)}), f32[32,64,256]{2,1,0:T(8,128)}, u32[]{:S(2)}, u32[]{:S(2)}) async-start(f32[32,64,256]{2,1,0:T(8,128)} %bitcast.257), calls=%async_computation.7 | async-start | bytes 4194304 | tf_op jit(solution)/shard_map/all_to_all | solution.py:141
  287.7 71.0 %all-to-all-start.8 = ((f32[32,64,256]{2,1,0:T(8,128)}), f32[32,64,256]{2,1,0:T(8,128)}, u32[]{:S(2)}, u32[]{:S(2)}) async-start(f32[32,64,256]{2,1,0:T(8,128)} %bitcast.255), calls=%async_computation.8 | async-start | bytes 4194304 | tf_op jit(solution)/shard_map/all_to_all | solution.py:142
  294.0 3.9 copy-start.4
  310.0 3.9 copy-start.5
  321.4 5.3 copy-start.14
  358.7 53.0 %all-to-all-start.4 = ((f32[64,32,256]{2,0,1:T(8,128)}), f32[64,32,256]{2,0,1:T(8,128)}, u32[]{:S(2)}, u32[]{:S(2)}) async-start(f32[64,32,256]{2,0,1:T(8,128)} %copy.149), calls=%async_computation.4 | async-start | bytes 4194304 | tf_op jit(solution)/shard_map/all_to_all | solution.py:161
  364.8 3.9 copy-start.3
  382.0 34.6 %copy-start.23 = (f32[4]{0:T(128)S(1)}, f32[4]{0:T(128)}, u32[]{:S(2)}) copy-start(f32[4]{0:T(128)} %param.17) | copy-start | bytes 52
  382.0 35.2 %copy-start.24 = (f32[4]{0:T(128)S(1)}, f32[4]{0:T(128)}, u32[]{:S(2)}) copy-start(f32[4]{0:T(128)} %param.18) | copy-start | bytes 52
  382.0 35.9 %copy-start.25 = (f32[4]{0:T(128)S(1)}, f32[4]{0:T(128)}, u32[]{:S(2)}) copy-start(f32[4]{0:T(128)} %param.19) | copy-start | bytes 52
  382.0 36.6 %copy-start.19 = (s32[1024,512]{1,0:T(8,128)S(1)}, s32[1024,512]{1,0:T(8,128)}, u32[]{:S(2)}) copy-start(s32[1024,512]{1,0:T(8,128)} %param.16) | copy-start | bytes 6291460
  411.7 51.4 %all-to-all-start.3 = ((f32[64,32,256]{2,0,1:T(8,128)}), f32[64,32,256]{2,0,1:T(8,128)}, u32[]{:S(2)}, u32[]{:S(2)}) async-start(f32[64,32,256]{2,0,1:T(8,128)} %copy.146), calls=%async_computation.3 | async-start | bytes 4194304 | tf_op jit(solution)/shard_map/all_to_all | solution.py:160
  426.6 7.9 %copy-start.13 = (f32[64,64,128]{2,1,0:T(8,128)}, f32[64,64,128]{2,1,0:T(8,128)S(1)}, u32[]{:S(2)}) copy-start(f32[64,64,128]{2,1,0:T(8,128)S(1)} %reshape.268) | copy-start | bytes 6291460
  463.0 5.5 copy-start.17
  483.0 54.7 %all-to-all-start.5 = ((f32[256,4,512]{0,2,1:T(8,128)}), f32[256,4,512]{0,2,1:T(8,128)}, u32[]{:S(2)}, u32[]{:S(2)}) async-start(f32[256,4,512]{0,2,1:T(8,128)} %bitcast.258), calls=%async_computation.5 | async-start | bytes 4194304 | tf_op jit(solution)/shard_map/all_to_all | solution.py:164
  488.3 3.8 copy-start.9
  504.8 3.9 copy-start.1
  537.8 3.0 copy-start.20
  537.8 3.0 copy-start.21
  537.8 3.0 copy-start.22
  (10 other events, 23.6 us)
where the time goes:
time: 590 us; the launch traced here: 582 us
  waiting for transfers between devices  173 us (29%)
  matrix products  136 us (23%)
  local copies, waits for them, and re-layouts  106 us (18%)
  other arithmetic  69.7 us (12%)
  blocking collectives  54.6 us (9%)
  starting transfers between devices  40.7 us (7%)
    dot_general x42, matrix products, product(): jnp.einsum(pattern, left_op, right_op, precision=lax.Precision.HIGHEST)  136 us
    all_to_all x1, blocking collectives, per_device(): lax.all_to_all(slip_rate, 'dip', split_axis=0, concat_axis=1, tiled=True)  54.6 us
    add x1, other arithmetic, friction(): state + time_step * (coef_b / length_l) * (jnp.exp(-state / coef_b) - jnp...  40.4 us
    all_to_all x1, waiting for transfers between devices, per_device(): lax.all_to_all(slip_im, ('strike', 'dip'), split_axis=0, concat_axis=1, t...  37.2 us
    all_to_all x1, waiting for transfers between devices, per_device(): lax.all_to_all(slip_re, ('strike', 'dip'), split_axis=0, concat_axis=1, t...  36.8 us
    all_to_all x1, waiting for transfers between devices, per_device(): lax.all_to_all(slip, 'dip', split_axis=0, concat_axis=1, tiled=True)  36.1 us
    mul x9, local copies, waits for them, and re-layouts, transform_rows(): part_im.reshape(out_shape) * factor  30.7 us
    mul x9, local copies, waits for them, and re-layouts, transform_rows(): part_re.reshape(out_shape) * factor  29.7 us
  transfers between devices with their start and end apart: 8, of which 6 were waited for; matrix products, arithmetic and copies ran while one was open for 39% of the time, Pallas kernels for 0%

commit v1 on v0

--- a/solution.py
+++ b/solution.py
@@ -9,6 +9,13 @@
 damping = 0.5
 relaxation = 0.35
 time_step = 0.1
+
+
+def trade_parts(x, mesh_axis, split, join):
+    size = lax.axis_size(mesh_axis)
+    blocks = jnp.stack(jnp.split(x, size, axis=split), axis=0)
+    blocks = lax.all_to_all(blocks, mesh_axis, split_axis=0, concat_axis=0)
+    return jnp.concatenate(blocks, axis=join)
 
 
 def inverse_sinh(value):
@@ -137,7 +144,7 @@
     rate_re, rate_im = transform_rows(rate_rows, None, -1.0, True)
     pieces = (
         lax.all_to_all(slip_re, ("strike", "dip"), split_axis=0, concat_axis=1, tiled=True),
-        lax.all_to_all(slip_im, ("strike", "dip"), split_axis=0, concat_axis=1, tiled=True),
+        trade_parts(slip_im, ("strike", "dip"), 0, 1),
         lax.all_to_all(rate_re, ("strike", "dip"), split_axis=0, concat_axis=1, tiled=True),
         lax.all_to_all(rate_im, ("strike", "dip"), split_axis=0, concat_axis=1, tiled=True),
     )

time: 590 us -> 608 us (1.031)
  local copies, waits for them, and re-layouts: 106 us -> 124 us
    unnamed x54 -> x85, local copies, waits for them, and re-layouts: 1.9 us -> 21.5 us
    mul x9 -> x8, local copies, waits for them, and re-layouts: 30.7 us -> 28.2 us  [transform_rows(): part_im.reshape(out_shape) * factor]
  transfers between devices with their start and end apart: 8 -> 8, of which waited for: 6 -> 6; matrix products, arithmetic and copies ran while one was open for 39% -> 37% of each run, Pallas kernels for 0% -> 0%
where the time goes in v1:
time: 608 us; the launch traced here: 601 us
  waiting for transfers between devices  173 us (28%)
  matrix products  136 us (22%)
  local copies, waits for them, and re-layouts  124 us (20%)
  other arithmetic  69.7 us (11%)
  blocking collectives  54.6 us (9%)
  starting transfers between devices  40.7 us (7%)
    dot_general x42, matrix products, product(): jnp.einsum(pattern, left_op, right_op, precision=lax.Precision.HIGHEST)  136 us
    all_to_all x1, blocking collectives, per_device(): lax.all_to_all(slip_rate, 'dip', split_axis=0, concat_axis=1, tiled=True)  54.6 us
    add x1, other arithmetic, friction(): state + time_step * (coef_b / length_l) * (jnp.exp(-state / coef_b) - jnp...  40.4 us
    all_to_all x1, waiting for transfers between devices, trade_parts(): blocks = lax.all_to_all(blocks, mesh_axis, split_axis=0, concat_axis=0)  37.2 us
    all_to_all x1, waiting for transfers between devices, per_device(): lax.all_to_all(slip_re, ('strike', 'dip'), split_axis=0, concat_axis=1, t...  36.8 us
    all_to_all x1, waiting for transfers between devices, per_device(): lax.all_to_all(slip, 'dip', split_axis=0, concat_axis=1, tiled=True)  36.1 us
    mul x9, local copies, waits for them, and re-layouts, transform_rows(): part_re.reshape(out_shape) * factor  29.7 us
    all_to_all x1, waiting for transfers between devices, per_device(): lax.all_to_all(back_im, ('strike', 'dip'), split_axis=1, concat_axis=0, t...  29.6 us
  transfers between devices with their start and end apart: 8, of which 6 were waited for; matrix products, arithmetic and copies ran while one was open for 37% of the time, Pallas kernels for 0%

profile of v1, /device:TPU:0, one launch (start us, length us, event | category | flops | bytes accessed | tf_op | source)
XLA Modules:
  0.0 600.6 jit_solution(8060377563121567887)
XLA Ops:
  0.6 54.6 %all_to_all.118 = f32[4,256,512]{2,1,0:T(8,128)S(1)} all-to-all(f32[4,256,512]{2,1,0:T(8,128)} %bitcast.356), channel_id=1, replica_groups=mesh['strike'=8,'dip'=4] {'dip'}, dimensions={0} | all-to-all | bytes 4194304 | tf_op jit(solution)/shard_map/all_to_all | solution.py:141
  71.0 36.1 %all-to-all-done = f32[4,256,512]{2,1,0:T(8,128)} async-done(((f32[4,256,512]{2,1,0:T(8,128)}), f32[4,256,512]{2,1,0:T(8,128)}, u32[]{:S(2)}, u32[]{:S(2)}) %all-to-all-start) | async-done | bytes 2097184 | tf_op jit(solution)/shard_map/all_to_all | solution.py:140
  116.9 5.5 subtract_bitcast_fusion
  163.1 37.2 %all-to-all-done.2 = f32[32,64,256]{2,1,0:T(8,128)} async-done(((f32[32,64,256]{2,1,0:T(8,128)}), f32[32,64,256]{2,1,0:T(8,128)}, u32[]{:S(2)}, u32[]{:S(2)}) %all-to-all-start.2) | async-done | bytes 2097184 | tf_op jit(solution)/shard_map/all_to_all | solution.py:17
  200.2 4.7 all-to-all-start.1
  214.8 36.8 %all-to-all-done.1 = f32[32,64,256]{2,1,0:T(8,128)} async-done(((f32[32,64,256]{2,1,0:T(8,128)}), f32[32,64,256]{2,1,0:T(8,128)}, u32[]{:S(2)}, u32[]{:S(2)}) %all-to-all-start.1) | async-done | bytes 2097184 | tf_op jit(solution)/shard_map/all_to_all | solution.py:146
  251.6 5.2 all-to-all-start.7
  256.8 20.0 %fusion.1 = (f32[64,8192]{1,0:T(8,128)}, f32[64,8192]{1,0:T(8,128)}) fusion(bf16[16,64,8192]{2,1,0:T(8,128)(2,1)} %param.20, bf16[16,2,64,8192]{3,2,1,0:T(8,128)(2,1)} %param.21), kind=kLoop, calls=%fused_computation.3 | loop fusion | flops 57671680 | bytes 54525952 | tf_op jit(solution)/shard_map/jrc,jrc->rc/dot_general | solution.py:160
  306.6 6.2 %all-to-all-start.8 = ((f32[32,64,256]{2,1,0:T(8,128)}), f32[32,64,256]{2,1,0:T(8,128)}, u32[]{:S(2)}, u32[]{:S(2)}) async-start(f32[32,64,256]{2,1,0:T(8,128)} %bitcast.350), calls=%async_computation.8 | async-start | bytes 4194304 | tf_op jit(solution)/shard_map/all_to_all | solution.py:149
  324.2 4.8 mul.981
  340.3 5.3 mul.985
  368.6 4.8 mul.997
  377.6 6.1 %all-to-all-start.4 = ((f32[64,32,256]{2,0,1:T(8,128)}), f32[64,32,256]{2,0,1:T(8,128)}, u32[]{:S(2)}, u32[]{:S(2)}) async-start(f32[64,32,256]{2,0,1:T(8,128)} %copy.242), calls=%async_computation.4 | async-start | bytes 4194304 | tf_op jit(solution)/shard_map/all_to_all | solution.py:168
  400.9 29.6 %all-to-all-done.4 = f32[64,32,256]{2,0,1:T(8,128)} async-done(((f32[64,32,256]{2,0,1:T(8,128)}), f32[64,32,256]{2,0,1:T(8,128)}, u32[]{:S(2)}, u32[]{:S(2)}) %all-to-all-start.4) | async-done | bytes 2097184 | tf_op jit(solution)/shard_map/all_to_all | solution.py:168
  430.6 4.7 all-to-all-start.3
  445.6 4.9 copy.266
  457.7 5.7 fusion.91
  463.4 5.7 fusion.89
  469.2 12.8 %all-to-all-done.3 = f32[64,32,256]{2,0,1:T(8,128)} async-done(((f32[64,32,256]{2,0,1:T(8,128)}), f32[64,32,256]{2,0,1:T(8,128)}, u32[]{:S(2)}, u32[]{:S(2)}) %all-to-all-start.3) | async-done | bytes 2097184 | tf_op jit(solution)/shard_map/all_to_all | solution.py:167
  481.9 5.5 fusion.109
  487.4 5.3 multiply_subtract_fusion.1
  501.9 5.3 all-to-all-start.5
  536.2 20.5 %all-to-all-done.5 = f32[256,4,512]{0,2,1:T(8,128)} async-done(((f32[256,4,512]{0,2,1:T(8,128)}), f32[256,4,512]{0,2,1:T(8,128)}, u32[]{:S(2)}, u32[]{:S(2)}) %all-to-all-start.5) | async-done | bytes 2097184 | tf_op jit(solution)/shard_map/all_to_all | solution.py:171
  559.7 40.4 %multiply_add_fusion.1 = (f32[1024,512]{1,0:T(8,128)}, f32[1024,512]{1,0:T(8,128)}) fusion(f32[1024,512]{1,0:T(8,128)} %param.13, pred[1024,512]{1,0:T(8,128)(4,1)} %get-tuple-element.48, pred[1024,512]{1,0:T(8,128)(4,1)S(1)} %copy-done.22, pred[1024,512]{1,0:T(8,128)(4,1)} %get-tuple-element.49, pred[1024,512]{1,0:T(8,128)(4,1)S(1)} %copy-done.21, ...), kind=kLoop, calls=%fused_computation.102 | loop fusion | flops 120061952 | bytes 16777264 | tf_op jit(solution)/shard_map/add | solution.py:118
  (202 shorter events, 230.8 us)
Async XLA Ops:
  55.2 51.9 %all-to-all-start = ((f32[4,256,512]{2,1,0:T(8,128)}), f32[4,256,512]{2,1,0:T(8,128)}, u32[]{:S(2)}, u32[]{:S(2)}) async-start(f32[4,256,512]{2,1,0:T(8,128)} %bitcast.355), calls=%async_computation | async-start | bytes 4194304 | tf_op jit(solution)/shard_map/all_to_all | solution.py:140
  149.3 50.9 %all-to-all-start.2 = ((f32[32,64,256]{2,1,0:T(8,128)}), f32[32,64,256]{2,1,0:T(8,128)}, u32[]{:S(2)}, u32[]{:S(2)}) async-start(f32[32,64,256]{2,1,0:T(8,128)} %constant_dynamic-update-slice_fusion), calls=%async_computation.2 | async-start | bytes 4194304 | tf_op jit(solution)/shard_map/all_to_all | solution.py:17
  153.4 4.4 copy-start.7
  200.2 51.4 %all-to-all-start.1 = ((f32[32,64,256]{2,1,0:T(8,128)}), f32[32,64,256]{2,1,0:T(8,128)}, u32[]{:S(2)}, u32[]{:S(2)}) async-start(f32[32,64,256]{2,1,0:T(8,128)} %bitcast.351), calls=%async_computation.1 | async-start | bytes 4194304 | tf_op jit(solution)/shard_map/all_to_all | solution.py:146
  251.6 55.0 %all-to-all-start.7 = ((f32[32,64,256]{2,1,0:T(8,128)}), f32[32,64,256]{2,1,0:T(8,128)}, u32[]{:S(2)}, u32[]{:S(2)}) async-start(f32[32,64,256]{2,1,0:T(8,128)} %bitcast.352), calls=%async_computation.7 | async-start | bytes 4194304 | tf_op jit(solution)/shard_map/all_to_all | solution.py:148
  306.6 71.0 %all-to-all-start.8 = ((f32[32,64,256]{2,1,0:T(8,128)}), f32[32,64,256]{2,1,0:T(8,128)}, u32[]{:S(2)}, u32[]{:S(2)}) async-start(f32[32,64,256]{2,1,0:T(8,128)} %bitcast.350), calls=%async_computation.8 | async-start | bytes 4194304 | tf_op jit(solution)/shard_map/all_to_all | solution.py:149
  312.8 3.9 copy-start.4
  328.9 3.9 copy-start.5
  340.3 5.3 copy-start.14
  377.6 53.0 %all-to-all-start.4 = ((f32[64,32,256]{2,0,1:T(8,128)}), f32[64,32,256]{2,0,1:T(8,128)}, u32[]{:S(2)}, u32[]{:S(2)}) async-start(f32[64,32,256]{2,0,1:T(8,128)} %copy.242), calls=%async_computation.4 | async-start | bytes 4194304 | tf_op jit(solution)/shard_map/all_to_all | solution.py:168
  383.7 3.9 copy-start.3
  400.9 34.6 %copy-start.23 = (f32[4]{0:T(128)S(1)}, f32[4]{0:T(128)}, u32[]{:S(2)}) copy-start(f32[4]{0:T(128)} %param.17) | copy-start | bytes 52
  400.9 35.3 %copy-start.24 = (f32[4]{0:T(128)S(1)}, f32[4]{0:T(128)}, u32[]{:S(2)}) copy-start(f32[4]{0:T(128)} %param.18) | copy-start | bytes 52
  400.9 35.9 %copy-start.25 = (f32[4]{0:T(128)S(1)}, f32[4]{0:T(128)}, u32[]{:S(2)}) copy-start(f32[4]{0:T(128)} %param.19) | copy-start | bytes 52
  400.9 36.6 %copy-start.19 = (s32[1024,512]{1,0:T(8,128)S(1)}, s32[1024,512]{1,0:T(8,128)}, u32[]{:S(2)}) copy-start(s32[1024,512]{1,0:T(8,128)} %param.16) | copy-start | bytes 6291460
  430.6 51.4 %all-to-all-start.3 = ((f32[64,32,256]{2,0,1:T(8,128)}), f32[64,32,256]{2,0,1:T(8,128)}, u32[]{:S(2)}, u32[]{:S(2)}) async-start(f32[64,32,256]{2,0,1:T(8,128)} %copy.239), calls=%async_computation.3 | async-start | bytes 4194304 | tf_op jit(solution)/shard_map/all_to_all | solution.py:167
  445.6 7.9 %copy-start.13 = (f32[64,64,128]{2,1,0:T(8,128)}, f32[64,64,128]{2,1,0:T(8,128)S(1)}, u32[]{:S(2)}) copy-start(f32[64,64,128]{2,1,0:T(8,128)S(1)} %reshape.327) | copy-start | bytes 6291460
  481.9 5.5 copy-start.17
  501.9 54.7 %all-to-all-start.5 = ((f32[256,4,512]{0,2,1:T(8,128)}), f32[256,4,512]{0,2,1:T(8,128)}, u32[]{:S(2)}, u32[]{:S(2)}) async-start(f32[256,4,512]{0,2,1:T(8,128)} %bitcast.353), calls=%async_computation.5 | async-start | bytes 4194304 | tf_op jit(solution)/shard_map/all_to_all | solution.py:171
  507.2 3.8 copy-start.9
  523.7 3.9 copy-start.1
  556.7 3.0 copy-start.20
  556.7 3.0 copy-start.21
  556.7 3.0 copy-start.22
  (10 other events, 23.6 us)
